TPU v7x, 32 devices: a whole 2x2x4 slice. The times are simulated.
32 devices in a mesh: row: 4 (over z), col: 8 (over y, x, core).
Axes of the slice: x: 2, y: 2, z: 4, core: 2. Of those that a mesh axis runs over, the one named last changes fastest.
Arguments:
- panel_block: bfloat16 [3584, 1024], P(('row', 'col')), may hold values from -1.5 to 1.5
- diag_inverse: bfloat16 [2, 512, 512], replicated
- trailing: bfloat16 [3584, 3584], P('row', 'col'), may hold values from -6 to 6
Outputs:
- factor_panel: bfloat16 [3584, 1024], P(('row', 'col'))
- updated: bfloat16 [3584, 3584], P('row', 'col')
All inputs are finite; a program needn't handle non-finite values.
Results may differ from a plain program's by a relative error of at most 0.0054.
Values may be sent and summed in bfloat16 or wider, within the bound.
No kernel may reach another device: no remote copies, remote signals or barrier semaphores. Data moves between devices by JAX's collectives and lax.ppermute only.
A program may use at most 128 MiB of HBM per device.

v0:
```python
import jax
import jax.numpy as jnp
from jax import lax
from jax.sharding import PartitionSpec as P

NB = 512
PANELS = 2


def body(panel_block, diag_inverse, trailing):
    pieces = []
    for panel in range(PANELS):
        columns = panel_block[:, panel * NB : (panel + 1) * NB]
        pieces.append(
            jnp.dot(
                columns, jnp.tril(diag_inverse[panel]).T, preferred_element_type=jnp.float32
            ).astype(jnp.bfloat16)
        )
    factor = jnp.concatenate(pieces, axis=1)
    column_block = lax.all_gather(factor, "row", axis=0, tiled=True)
    product = lax.dot_general(
        lax.all_gather(factor, "col", axis=0, tiled=True),
        column_block,
        (((1,), (1,)), ((), ())),
        preferred_element_type=jnp.float32,
    )
    updated = (trailing.astype(jnp.float32) - product).astype(jnp.bfloat16)
    return (factor, updated)


def solution(mesh):
    placed = (P(("row", "col"), None), P(), P("row", "col"))
    return jax.shard_map(
        body,
        mesh=mesh,
        in_specs=placed,
        out_specs=(P(("row", "col"), None), P("row", "col")),
        check_vma=False,
    )
```

profile of v0, /device:TPU:0, one launch (start us, length us, event | category | flops | bytes accessed | tf_op | source)
XLA Modules:
  0.0 50.7 jit_solution(15420570001928043518)
XLA Ops:
  7.2 0.0 all-gather.2.cloned.1.call-start
  7.2 1.3 %fusion.1 = bf16[112,512]{1,0:T(8,128)(2,1)S(1)} fusion(bf16[2,512,512]{2,1,0:T(8,128)(2,1)} %param.4, bf16[112,1024]{1,0:T(8,128)(2,1)} %param.3), kind=kOutput, calls=%fused_computation.4 | convolution fusion | flops 59301888 | bytes 753664 | tf_op jit(solution)/shard_map/dot_general | solution.py:15
  8.6 0.0 copy-start
  8.6 1.4 %fusion = bf16[112,512]{1,0:T(8,128)(2,1)S(1)} fusion(bf16[2,512,512]{2,1,0:T(8,128)(2,1)} %param.4, bf16[112,1024]{1,0:T(8,128)(2,1)} %param.3), kind=kOutput, calls=%fused_computation.3 | convolution fusion | flops 59301888 | bytes 753664 | tf_op jit(solution)/shard_map/dot_general | solution.py:15
  10.0 0.7 %pad_maximum_fusion = bf16[112,1024]{1,0:T(8,128)(2,1)} fusion(bf16[112,512]{1,0:T(8,128)(2,1)S(1)} %fusion.1, bf16[112,512]{1,0:T(8,128)(2,1)S(1)} %fusion), kind=kLoop, calls=%fused_computation.14 | loop fusion | flops 458752 | bytes 458752 | tf_op jit(solution)/shard_map/concatenate | solution.py:19
  10.7 0.0 all-gather.2.cloned.1.call-update
  10.7 23.0 %all_gather.7 = bf16[448,1024]{1,0:T(8,128)(2,1)S(1)} all-gather(bf16[112,1024]{1,0:T(8,128)(2,1)} %pad_maximum_fusion), channel_id=1, replica_groups=mesh['row'=4,'col'=8] {'row'}, dimensions={0}, use_global_device_ids=true | all-gather | bytes 1146880 | tf_op jit(solution)/shard_map/all_gather | solution.py:20
  33.7 6.6 %all-gather.2.cloned.1.call-done = bf16[896,1024]{1,0:T(8,128)(2,1)} async-done(((bf16[112,1024]{1,0:T(8,128)(2,1)}), bf16[896,1024]{1,0:T(8,128)(2,1)}) %all-gather.2.cloned.1.call-update) | async-done | bytes 1835024 | tf_op jit(solution)/shard_map/all_gather | solution.py:22
  40.3 0.0 copy-done
  40.3 3.5 %subtract_convert_fusion = bf16[896,448]{0,1:T(8,128)(2,1)} fusion(bf16[896,448]{0,1:T(8,128)(2,1)S(1)} %copy-done, bf16[896,1024]{1,0:T(8,128)(2,1)} %all-gather.2.cloned.1.call-done, bf16[448,1024]{1,0:T(8,128)(2,1)S(1)} %all_gather.7), kind=kOutput, calls=%fused_computation | convolution fusion | flops 823287808 | bytes 4358144 | tf_op jit(solution)/shard_map/dot_general | solution.py:21
Async XLA Ops:
  7.2 33.1 %all-gather.2.cloned.1.call-start = ((), (), s32[]{:S(2)}) async-start(), calls=%async_computation | async-start | bytes 2064384 | tf_op jit(solution)/shard_map/all_gather | solution.py:22
  8.6 31.7 %copy-start = (bf16[896,448]{0,1:T(8,128)(2,1)S(1)}, bf16[896,448]{0,1:T(8,128)(2,1)}, u32[]{:S(2)}) copy-start(bf16[896,448]{0,1:T(8,128)(2,1)} %param.5) | copy-start | bytes 2408452
Sparse Core Ops, SparseCore 0:
  10.8 29.3 all-gather.1
where the time goes:
time: 50.9 us; the launch traced here: 50.7 us
  blocking collectives  23 us (45%)
  between operations  14.1 us (28%)
  waiting for transfers between devices  6.61 us (13%)
  matrix products  6.29 us (12%)
  other arithmetic  0.71 us (1%)
    all_gather x1, blocking collectives, body(): column_block = lax.all_gather(factor, 'row', axis=0, tiled=True)  23 us
    all_gather x1, waiting for transfers between devices, body(): lax.all_gather(factor, 'col', axis=0, tiled=True)  6.59 us
    dot_general x1, matrix products, body(): lax.dot_general(lax.all_gather(factor, 'col', axis=0, tiled=True), column...  3.54 us
    dot_general x2, matrix products, body(): jnp.dot(columns, jnp.tril(diag_inverse[panel]).T, preferred_element_type=...  2.75 us
  transfers between devices with their start and end apart: 1, of which 1 were waited for; matrix products, arithmetic and copies ran while one was open for 0% of the time, Pallas kernels for 0%

commit v1 on v0

--- a/solution.py
+++ b/solution.py
@@ -5,6 +5,18 @@
 
 NB = 512
 PANELS = 2
+
+
+def doubled_up(array, axis, dim):
+    ways, here = (lax.axis_size(axis), lax.axis_index(axis))
+    grown, reach = (array, 1)
+    while reach < ways:
+        theirs = lax.ppermute(grown, axis, [(d, d ^ reach) for d in range(ways)])
+        mine_first = jnp.concatenate([grown, theirs], axis=dim)
+        theirs_first = jnp.concatenate([theirs, grown], axis=dim)
+        grown = jnp.where(here & reach == 0, mine_first, theirs_first)
+        reach = 2 * reach
+    return grown
 
 
 def body(panel_block, diag_inverse, trailing):
@@ -19,7 +31,7 @@
     factor = jnp.concatenate(pieces, axis=1)
     column_block = lax.all_gather(factor, "row", axis=0, tiled=True)
     product = lax.dot_general(
-        lax.all_gather(factor, "col", axis=0, tiled=True),
+        doubled_up(factor, "col", 0),
         column_block,
         (((1,), (1,)), ((), ())),
         preferred_element_type=jnp.float32,

time: 50.9 us -> 43.7 us (0.86)
  between operations: 14.1 us -> 0.71 us
  waiting for transfers between devices: 6.61 us -> 11.9 us
  starting transfers between devices: 0.04 us -> 5.31 us
  matrix products: 6.29 us -> 3.79 us
  blocking collectives: 23 us -> 21.3 us
    ppermute x0 -> x3, waiting for transfers between devices: none -> 11.9 us  [doubled_up(): theirs = lax.ppermute(grown, axis, [(d, d ^ reach) for d in range(ways)])]
    all_gather x1 -> x0, waiting for transfers between devices: 6.59 us -> none  [body(): lax.all_gather(factor, 'col', axis=0, tiled=True)]
    ppermute x0 -> x3, starting transfers between devices: none -> 5.31 us  [doubled_up(): theirs = lax.ppermute(grown, axis, [(d, d ^ reach) for d in range(ways)])]
    all_gather x1, blocking collectives: 23 us -> 21.3 us  [body(): column_block = lax.all_gather(factor, 'row', axis=0, tiled=True)]
    dot_general x1, matrix products: 3.54 us -> 2.07 us  [body(): lax.dot_general(doubled_up(factor, 'col', 0), column_block, (((1,), (1,))...]
    dot_general x2, matrix products: 2.75 us -> 1.72 us  [body(): jnp.dot(columns, jnp.tril(diag_inverse[panel]).T, preferred_element_type=...]
    concatenate x1, other arithmetic: 0.71 us -> 0.02 us  [body(): factor = jnp.concatenate(pieces, axis=1)]
  transfers between devices with their start and end apart: 1 -> 3, of which waited for: 1 -> 2; matrix products, arithmetic and copies ran while one was open for 0% -> 0% of each run, Pallas kernels for 0% -> 0%
where the time goes in v1:
time: 43.7 us; the launch traced here: 43.5 us
  blocking collectives  21.3 us (49%)
  waiting for transfers between devices  11.9 us (27%)
  starting transfers between devices  5.31 us (12%)
  matrix products  3.79 us (9%)
  between operations  0.71 us (2%)
  other arithmetic  0.48 us (1%)
    all_gather x1, blocking collectives, body(): column_block = lax.all_gather(factor, 'row', axis=0, tiled=True)  21.3 us
    ppermute x3, waiting for transfers between devices, doubled_up(): theirs = lax.ppermute(grown, axis, [(d, d ^ reach) for d in range(ways)])  11.9 us
    ppermute x3, starting transfers between devices, doubled_up(): theirs = lax.ppermute(grown, axis, [(d, d ^ reach) for d in range(ways)])  5.31 us
    dot_general x1, matrix products, body(): lax.dot_general(doubled_up(factor, 'col', 0), column_block, (((1,), (1,))...  2.07 us
    dot_general x2, matrix products, body(): jnp.dot(columns, jnp.tril(diag_inverse[panel]).T, preferred_element_type=...  1.72 us
  transfers between devices with their start and end apart: 3, of which 2 were waited for; matrix products, arithmetic and copies ran while one was open for 0% of the time, Pallas kernels for 0%

profile of v1, /device:TPU:0, one launch (start us, length us, event | category | flops | bytes accessed | tf_op | source)
XLA Modules:
  0.0 43.5 jit_solution(16403604282638373129)
XLA Ops:
  0.6 0.0 copy-start.1
  0.6 0.0 copy-start.3
  0.6 1.4 %fusion.8 = bf16[112,512]{1,0:T(8,128)(2,1)S(1)} fusion(bf16[2,512,512]{2,1,0:T(8,128)(2,1)} %param.4, bf16[112,1024]{1,0:T(8,128)(2,1)} %param.3), kind=kOutput, calls=%fused_computation.12 | convolution fusion | flops 59301888 | bytes 753664 | tf_op jit(solution)/shard_map/dot_general | solution.py:27
  2.1 0.0 copy-done.1
  2.1 0.0 copy-done.3
  2.1 0.3 fusion.7
  2.4 0.0 copy-start
  2.4 0.6 %collective-permute-start = (bf16[112,1024]{1,0:T(8,128)(2,1)S(1)}, bf16[112,1024]{1,0:T(8,128)(2,1)S(1)}, u32[]{:S(2)}, u32[]{:S(2)}) collective-permute-start(bf16[112,1024]{1,0:T(8,128)(2,1)S(1)} %pad_maximum_fusion), channel_id=1, source_target_pairs={{0,1},{1,0},{2,3},{3,2},{4,5},{5,4},{6,7},{7,6},{8,9},{9,8},{10,11... | collective-permute-start | bytes 688136 | tf_op jit(solution)/shard_map/ppermute | solution.py:14
  3.0 1.1 %collective-permute-done = bf16[112,1024]{1,0:T(8,128)(2,1)S(1)} collective-permute-done((bf16[112,1024]{1,0:T(8,128)(2,1)S(1)}, bf16[112,1024]{1,0:T(8,128)(2,1)S(1)}, u32[]{:S(2)}, u32[]{:S(2)}) %collective-permute-start) | collective-permute-done | bytes 229408 | tf_op jit(solution)/shard_map/ppermute | solution.py:14
  4.1 0.1 maximum_select_fusion.5
  4.2 2.9 %collective-permute-start.1 = (bf16[224,1024]{1,0:T(8,128)(2,1)S(1)}, bf16[224,1024]{1,0:T(8,128)(2,1)S(1)}, u32[]{:S(2)}, u32[]{:S(2)}) collective-permute-start(bf16[224,1024]{1,0:T(8,128)(2,1)S(1)} %maximum_select_fusion.5), channel_id=1, source_target_pairs={{0,2},{1,3},{2,0},{3,1},{4,6},{5,7},{6,4},{7,5},{8,10},{9,11},{10,... | collective-permute-start | bytes 1376264 | tf_op jit(solution)/shard_map/ppermute | solution.py:14
  7.1 0.0 copy-start.2
  7.1 10.8 %collective-permute-done.1 = bf16[224,1024]{1,0:T(8,128)(2,1)S(1)} collective-permute-done((bf16[224,1024]{1,0:T(8,128)(2,1)S(1)}, bf16[224,1024]{1,0:T(8,128)(2,1)S(1)}, u32[]{:S(2)}, u32[]{:S(2)}) %collective-permute-start.1) | collective-permute-done | bytes 458784 | tf_op jit(solution)/shard_map/ppermute | solution.py:14
  18.0 0.4 maximum_select_fusion.4
  18.3 1.8 %collective-permute-start.2 = (bf16[448,1024]{1,0:T(8,128)(2,1)S(1)}, bf16[448,1024]{1,0:T(8,128)(2,1)S(1)}, u32[]{:S(2)}, u32[]{:S(2)}) collective-permute-start(bf16[448,1024]{1,0:T(8,128)(2,1)S(1)} %maximum_select_fusion.4), channel_id=1, source_target_pairs={{0,4},{1,5},{2,6},{3,7},{4,0},{5,1},{6,2},{7,3},{8,12},{9,13},{10,... | collective-permute-start | bytes 2752520 | tf_op jit(solution)/shard_map/ppermute | solution.py:14
  20.2 0.0 copy-done
  20.2 21.3 %all_gather.3 = bf16[448,1024]{1,0:T(8,128)(2,1)S(1)} all-gather(bf16[112,1024]{1,0:T(8,128)(2,1)S(1)} %pad_maximum_fusion), channel_id=1, replica_groups=mesh['row'=4,'col'=8] {'row'}, dimensions={0}, use_global_device_ids=true | all-gather | bytes 1146880 | tf_op jit(solution)/shard_map/all_gather | solution.py:32
  41.4 0.0 collective-permute-done.2
  41.4 0.0 copy-done.2
  41.4 2.1 %subtract_convert_fusion = bf16[896,448]{0,1:T(8,128)(2,1)} fusion(bf16[896,448]{0,1:T(8,128)(2,1)S(1)} %copy-done.2, bf16[448,1024]{1,0:T(8,128)(2,1)S(1)} %all_gather.3, bf16[448,1024]{1,0:T(8,128)(2,1)S(1)} %collective-permute-done.2, bf16[448,1024]{1,0:T(8,128)(2,1)S(1)} %maximum_select_fusion.4, pred[]{:T(512)S(6)} %eq.9), kind=kOutput, calls=%fused_computation.8 | convolution fusion | flops 831545344 | bytes 4358145 | tf_op jit(solution)/shard_map/dot_general | solution.py:33
  (1 shorter events, 0.0 us)
Async XLA Ops:
  0.6 1.5 %copy-start.1 = (bf16[2,512,512]{2,1,0:T(8,128)(2,1)S(1)}, bf16[2,512,512]{2,1,0:T(8,128)(2,1)}, u32[]{:S(2)}) copy-start(bf16[2,512,512]{2,1,0:T(8,128)(2,1)} %param.4) | copy-start | bytes 3145732
  0.6 1.5 %copy-start.3 = (bf16[112,1024]{1,0:T(8,128)(2,1)S(1)}, bf16[112,1024]{1,0:T(8,128)(2,1)}, u32[]{:S(2)}) copy-start(bf16[112,1024]{1,0:T(8,128)(2,1)} %param.3) | copy-start | bytes 688132
  2.4 17.7 %copy-start = (bf16[112,1024]{1,0:T(8,128)(2,1)}, bf16[112,1024]{1,0:T(8,128)(2,1)S(1)}, u32[]{:S(2)}) copy-start(bf16[112,1024]{1,0:T(8,128)(2,1)S(1)} %pad_maximum_fusion) | copy-start | bytes 688132
  2.4 1.7 %collective-permute-start = (bf16[112,1024]{1,0:T(8,128)(2,1)S(1)}, bf16[112,1024]{1,0:T(8,128)(2,1)S(1)}, u32[]{:S(2)}, u32[]{:S(2)}) collective-permute-start(bf16[112,1024]{1,0:T(8,128)(2,1)S(1)} %pad_maximum_fusion), channel_id=1, source_target_pairs={{0,1},{1,0},{2,3},{3,2},{4,5},{5,4},{6,7},{7,6},{8,9},{9,8},{10,11... | collective-permute-start | bytes 688136 | tf_op jit(solution)/shard_map/ppermute | solution.py:14
  4.2 13.7 %collective-permute-start.1 = (bf16[224,1024]{1,0:T(8,128)(2,1)S(1)}, bf16[224,1024]{1,0:T(8,128)(2,1)S(1)}, u32[]{:S(2)}, u32[]{:S(2)}) collective-permute-start(bf16[224,1024]{1,0:T(8,128)(2,1)S(1)} %maximum_select_fusion.5), channel_id=1, source_target_pairs={{0,2},{1,3},{2,0},{3,1},{4,6},{5,7},{6,4},{7,5},{8,10},{9,11},{10,... | collective-permute-start | bytes 1376264 | tf_op jit(solution)/shard_map/ppermute | solution.py:14
  7.1 34.3 %copy-start.2 = (bf16[896,448]{0,1:T(8,128)(2,1)S(1)}, bf16[896,448]{0,1:T(8,128)(2,1)}, u32[]{:S(2)}) copy-start(bf16[896,448]{0,1:T(8,128)(2,1)} %param.5) | copy-start | bytes 2408452
  18.3 23.1 %collective-permute-start.2 = (bf16[448,1024]{1,0:T(8,128)(2,1)S(1)}, bf16[448,1024]{1,0:T(8,128)(2,1)S(1)}, u32[]{:S(2)}, u32[]{:S(2)}) collective-permute-start(bf16[448,1024]{1,0:T(8,128)(2,1)S(1)} %maximum_select_fusion.4), channel_id=1, source_target_pairs={{0,4},{1,5},{2,6},{3,7},{4,0},{5,1},{6,2},{7,3},{8,12},{9,13},{10,... | collective-permute-start | bytes 2752520 | tf_op jit(solution)/shard_map/ppermute | solution.py:14
